TPU v7x, 256 devices: a whole 4x4x8 slice. The times are simulated.
256 devices in a mesh: node: 16 (over z_lo, y), rep: 16 (over x, z_hi, core).
Axes of the slice: x: 4, y: 4, z: 8 (z_hi: 2, z_lo: 4; z = z_hi * 4 + z_lo), core: 2. Of those that a mesh axis runs over, the one named last changes fastest.
Arguments:
- tokens: bfloat16 [32768, 8192], P(('node', 'rep')), may hold values from -24 to 24
- norm_gain: float32 [8192], replicated, may hold values from 0.5 to 1.5
- key_cotangent: bfloat16 [32768, 512], P(('node', 'rep')), may hold values from -6 to 6
- secondary: bfloat16 [8192, 512], P('node'), may hold values from -0.0625 to 0.0625
- master: float32 [8192, 512], P(('node', 'rep')), may hold values from -0.0625 to 0.0625
- moment_first: float32 [4096, 1024], P(('node', 'rep')), may hold values from -0.03314563 to 0.03314563
- moment_second: float32 [4096, 1024], P(('node', 'rep')), may hold values from 7.6293945e-06 to 0.00012207031
- signs: int32 [1024], replicated, may hold values from 0 to 1
Outputs:
- keys: bfloat16 [32768, 512], P(('node', 'rep'))
- token_grad: bfloat16 [32768, 8192], P(('node', 'rep'))
- new_master: float32 [8192, 512], P(('node', 'rep'))
- new_first: float32 [4096, 1024], P(('node', 'rep'))
- new_second: float32 [4096, 1024], P(('node', 'rep'))
- new_secondary: bfloat16 [8192, 512], P('node')
All inputs are finite; a program needn't handle non-finite values.
Results may differ from a plain program's by a relative error of at most 0.0049.
Values may be sent and summed in bfloat16 or wider, within the bound.
No kernel may reach another device: no remote copies, remote signals or barrier semaphores. Data moves between devices by JAX's collectives and lax.ppermute only.
A program may use at most 128 MiB of HBM per device.

v0:
```python
import math
import jax
import jax.numpy as jnp
from jax import lax
from jax.sharding import PartitionSpec as P

PAIR_GAP = 16
norm_eps = 1e-05
adam_eps = 1e-08
beta_first = 0.9
beta_second = 0.95
adam_steps = 10
learn_rate = 0.002
weight_decay = 0.1


def split_up(value, dim, peers):
    dims = value.shape
    blocks = value.reshape(*dims[:dim], peers, dims[dim] // peers, *dims[dim + 1 :])
    return jnp.moveaxis(blocks, dim, 0)


def sent_and_summed(value, axis, dim):
    peers = lax.axis_size(axis)
    blocks = lax.all_to_all(split_up(value, dim, peers), axis, 0, 0, tiled=True)
    return jnp.sum(blocks.astype(jnp.float32), axis=0)


def sent_to_all(value, axis):
    copies = jnp.broadcast_to(value, (lax.axis_size(axis), *value.shape))
    return lax.all_to_all(copies, axis, split_axis=0, concat_axis=0, tiled=True)


def laid_out(blocks, dim):
    blocks = jnp.moveaxis(blocks, 0, dim)
    dims = blocks.shape
    return blocks.reshape(*dims[:dim], dims[dim] * dims[dim + 1], *dims[dim + 2 :])


def gathered_copies(value, axis, dim):
    blocks = sent_to_all(value, axis)
    return laid_out(blocks, dim)


def sylvester(extent):
    position = jnp.arange(extent, dtype=jnp.int32)
    parity = jnp.zeros((extent, extent), jnp.int32)
    for bit_place in range(extent.bit_length() - 1):
        parity = parity + (position[:, None] >> bit_place & 1) * (
            position[None, :] >> bit_place & 1
        )
    return (1 - 2 * (parity % 2)).astype(jnp.float32)


def shards(tokens, norm_gain, key_cotangent, secondary, master, moment_first, moment_second, signs):
    tok_rows, model_width = tokens.shape
    key_width = key_cotangent.shape[1]
    node_count = lax.axis_size("node")
    rep_count = lax.axis_size("rep")
    all_tokens = tok_rows * node_count * rep_count
    had_table = sylvester(key_width)
    sign_rows = (1 - 2 * signs).astype(jnp.float32).reshape(2, key_width)
    floats = tokens.astype(jnp.float32)
    inverse = lax.rsqrt(jnp.mean(floats * floats, axis=-1, keepdims=True) + norm_eps)
    normed = floats * inverse
    hidden = (normed * norm_gain).astype(jnp.bfloat16)
    gathered = lax.all_gather(secondary, "node", axis=0, tiled=True)
    keys = jnp.dot(hidden, gathered, preferred_element_type=jnp.float32).astype(jnp.bfloat16)
    hidden_grad = lax.dot_general(
        key_cotangent, gathered, (((1,), (1,)), ((), ())), preferred_element_type=jnp.float32
    )
    scaled = hidden_grad * norm_gain
    token_grad = (
        inverse * (scaled - normed * jnp.mean(scaled * normed, axis=-1, keepdims=True))
    ).astype(jnp.bfloat16)
    rot_scale = 1.0 / (math.sqrt(2 * key_width) * all_tokens)
    flipped = (key_cotangent[:, None, :] * sign_rows.astype(jnp.bfloat16)).reshape(
        2 * tok_rows, key_width
    )
    rotated = (
        jnp.dot(flipped, had_table.astype(jnp.bfloat16), preferred_element_type=jnp.float32)
        * rot_scale
    )
    rotated = rotated.astype(jnp.bfloat16).reshape(tok_rows, 2, key_width)
    amount = lax.axis_size("node") * (model_width // 2 // node_count)
    grouped = hidden.reshape(tok_rows, amount // PAIR_GAP, 2, PAIR_GAP)
    halves = jnp.einsum("tgaj,tak->agjk", grouped, rotated, preferred_element_type=jnp.float32)
    joined = jnp.concatenate([halves[0] + halves[1], halves[0] - halves[1]], axis=-1)
    partial_sum = lax.psum_scatter(
        joined.reshape(amount, 2 * key_width).astype(jnp.bfloat16),
        "node",
        scatter_dimension=0,
        tiled=True,
    )
    coded = sent_and_summed(partial_sum, "rep", 0)
    new_first = beta_first * moment_first + (1.0 - beta_first) * coded
    new_second = beta_second * moment_second + (1.0 - beta_second) * coded * coded
    first_hat = new_first / (1.0 - beta_first**adam_steps)
    second_hat = new_second / (1.0 - beta_second**adam_steps)
    ratio = first_hat / (jnp.sqrt(second_hat) + adam_eps)
    lower = ratio[:, :key_width]
    upper = ratio[:, key_width:]
    norm_root = math.sqrt(2 * key_width)
    row_even = jnp.dot(lower + upper, had_table) / norm_root * sign_rows[0]
    row_odd = jnp.dot(lower - upper, had_table) / norm_root * sign_rows[1]
    stacked = jnp.stack([row_even, row_odd], axis=1)
    master_rows = master.shape[0]
    update = (
        stacked.reshape(master_rows // (2 * PAIR_GAP), PAIR_GAP, 2, key_width)
        .transpose(0, 2, 1, 3)
        .reshape(master_rows, key_width)
    )
    new_master = master - learn_rate * (update + weight_decay * master)
    new_secondary = gathered_copies(new_master.astype(jnp.bfloat16), "rep", 0)
    return (keys, token_grad, new_master, new_first, new_second, new_secondary)


def solution(mesh):
    return jax.shard_map(
        shards,
        mesh=mesh,
        in_specs=(
            P(("node", "rep"), None),
            P(),
            P(("node", "rep"), None),
            P("node", None),
            P(("node", "rep"), None),
            P(("node", "rep"), None),
            P(("node", "rep"), None),
            P(),
        ),
        out_specs=(
            P(("node", "rep"), None),
            P(("node", "rep"), None),
            P(("node", "rep"), None),
            P(("node", "rep"), None),
            P(("node", "rep"), None),
            P("node", None),
        ),
        check_vma=False,
    )
```

profile of v0, /device:TPU:1, one launch (start us, length us, event | category | flops | bytes accessed | tf_op | source)
XLA Modules:
  0.0 313.9 jit_solution(15563459181511982867)
XLA Ops:
  7.2 0.0 all-gather.2.cloned.1.call-start
  7.2 0.7 all-gather.2.cloned.1.call-update
  7.9 0.0 reduce-scatter.2.cloned.1.call-start
  7.9 0.7 subtract_convert_fusion.1
  8.7 1.2 broadcast_multiply_fusion
  9.8 0.1 mul.382
  10.0 0.0 copy-start
  10.0 0.0 copy-start.2
  10.0 0.0 copy-start.3
  10.0 1.4 fusion.11
  11.5 0.1 reshape.197
  11.6 0.0 copy-done
  11.6 0.5 fusion.8
  12.1 104.0 %all-gather.2.cloned.1.call-done = bf16[8192,512]{1,0:T(8,128)(2,1)} async-done(((bf16[512,512]{1,0:T(8,128)(2,1)}), bf16[8192,512]{1,0:T(8,128)(2,1)}) %all-gather.2.cloned.1.call-update) | async-done | bytes 8388624 | tf_op jit(solution)/shard_map/all_gather | solution.py:67
  116.1 0.0 copy-done.2
  116.1 0.0 copy-done.3
  116.1 0.0 copy-start.1
  116.1 6.4 %fusion.4 = (f32[128]{0:T(128)S(1)}, f32[128,8192]{1,0:T(8,128)S(1)}) fusion(bf16[128,8192]{1,0:T(8,128)(2,1)S(1)} %copy-done, f32[128]{0:T(128)S(1)} %add_rsqrt_fusion, f32[8192]{0:T(1024)S(1)} %copy-done.3, bf16[128,512]{1,0:T(8,128)(2,1)S(1)} %copy-done.2, bf16[8192,512]{1,0:T(8,128)(2,1)} %all-gather.2.cloned.1.call-done), kind=kOutput, calls=%fused_computation.10 | convolution fusion | flops 1078984576 | bytes 14844928 | tf_op jit(solution)/shard_map/dot_general | solution.py:69
  122.6 0.0 copy-done.1
  122.6 2.5 fusion.7
  125.1 2.5 copy.16
  127.6 3.9 %fusion.9 = f32[2,256,16,512]{3,1,2,0:T(8,128)S(1)} fusion(bf16[128,256,2,16]{0,3,2,1:T(8,128)(2,1)} %bitcast.28, bf16[128,2,512,1]{2,1,0,3:T(2,128)(2,1)S(1)} %bitcast.30), kind=kOutput, calls=%fused_computation.15 | convolution fusion | flops 1073741824 | bytes 19136512 | tf_op jit(solution)/shard_map/tgaj,tak->agjk/dot_general | solution.py:87
  131.6 4.1 %add_convert_fusion = (bf16[1,256,16,512]{3,1,2,0:T(8,128)(2,1)}, bf16[1,256,16,512]{3,1,2,0:T(8,128)(2,1)S(1)}) fusion(f32[2,256,16,512]{3,1,2,0:T(8,128)S(1)} %fusion.9), kind=kLoop, calls=%fused_computation.3 | loop fusion | flops 8388608 | bytes 25165824 | tf_op jit(solution)/shard_map/convert.3
  135.7 6.5 %copy.19 = bf16[1,256,16,512]{3,2,1,0:T(8,128)(2,1)} copy(bf16[1,256,16,512]{3,1,2,0:T(8,128)(2,1)} %get-tuple-element.11) | data formatting | bytes 8388608 | tf_op jit(solution)/shard_map/convert.3
  142.2 4.3 %copy.20 = bf16[1,256,16,512]{3,2,1,0:T(8,128)(2,1)} copy(bf16[1,256,16,512]{3,1,2,0:T(8,128)(2,1)S(1)} %get-tuple-element.12) | data formatting | bytes 8388608 | tf_op jit(solution)/shard_map/convert.2
  146.5 7.9 %pad_maximum_fusion = bf16[4096,1024]{1,0:T(8,128)(2,1)} fusion(bf16[4096,512]{1,0:T(8,128)(2,1)} %bitcast.27, bf16[4096,512]{1,0:T(8,128)(2,1)} %bitcast.26), kind=kLoop, calls=%fused_computation.1 | loop fusion | flops 16777216 | bytes 16777216 | tf_op jit(solution)/shard_map/concatenate | solution.py:88
  154.4 0.0 copy-start.5
  154.4 0.0 copy-start.6
  154.4 0.0 reduce-scatter.2.cloned.1.call-update
  154.4 96.1 %reduce-scatter.2.cloned.1.call-done = bf16[256,1024]{1,0:T(8,128)(2,1)} async-done(((bf16[4096,1024]{1,0:T(8,128)(2,1)}), bf16[256,1024]{1,0:T(8,128)(2,1)}) %reduce-scatter.2.cloned.1.call-update) | async-done | bytes 524304 | tf_op jit(solution)/shard_map/reduce_scatter | solution.py:89
  250.5 15.8 %all-to-all-start = ((bf16[16,16,1024]{2,1,0:T(8,128)(2,1)}), bf16[16,16,1024]{2,1,0:T(8,128)(2,1)S(1)}, u32[]{:S(2)}, u32[]{:S(2)}) async-start(bf16[16,16,1024]{2,1,0:T(8,128)(2,1)} %bitcast.31), calls=%async_computation.1 | async-start | bytes 1048576 | tf_op jit(solution)/shard_map/all_to_all | solution.py:25
  266.3 13.7 %all-to-all-done = bf16[16,16,1024]{2,1,0:T(8,128)(2,1)S(1)} async-done(((bf16[16,16,1024]{2,1,0:T(8,128)(2,1)}), bf16[16,16,1024]{2,1,0:T(8,128)(2,1)S(1)}, u32[]{:S(2)}, u32[]{:S(2)}) %all-to-all-start) | async-done | bytes 524320 | tf_op jit(solution)/shard_map/all_to_all | solution.py:25
  280.0 0.1 convert_reduce_fusion
  280.1 0.0 copy-done.5
  280.1 0.0 copy-done.6
  280.1 0.7 add_divide_fusion
  280.8 1.3 fusion.13
  282.1 0.0 copy-start.4
  282.1 1.3 fusion.12
  283.4 0.0 copy-done.4
  283.4 0.6 fusion.42
  284.1 0.8 broadcast_in_dim.2
  284.9 7.7 %all-to-all-start.1 = ((bf16[16,32,512]{2,1,0:T(8,128)(2,1)}), bf16[16,32,512]{2,1,0:T(8,128)(2,1)S(1)}, u32[]{:S(2)}, u32[]{:S(2)}) async-start(bf16[16,32,512]{2,1,0:T(8,128)(2,1)} %broadcast_in_dim.2), calls=%async_computation.2 | async-start | bytes 1048576 | tf_op jit(solution)/shard_map/all_to_all | solution.py:31
  292.6 5.3 %convolution_convert_fusion = bf16[128,512]{1,0:T(8,128)(2,1)} fusion(bf16[128,8192]{1,0:T(8,128)(2,1)S(1)} %get-tuple-element.14, bf16[8192,512]{1,0:T(8,128)(2,1)} %all-gather.2.cloned.1.call-done), kind=kOutput, calls=%fused_computation.22 | convolution fusion | flops 1073807360 | bytes 10616832 | tf_op jit(solution)/shard_map/dot_general | solution.py:68
  297.9 8.4 %all-to-all-done.1 = bf16[16,32,512]{2,1,0:T(8,128)(2,1)S(1)} async-done(((bf16[16,32,512]{2,1,0:T(8,128)(2,1)}), bf16[16,32,512]{2,1,0:T(8,128)(2,1)S(1)}, u32[]{:S(2)}, u32[]{:S(2)}) %all-to-all-start.1) | async-done | bytes 524320 | tf_op jit(solution)/shard_map/all_to_all | solution.py:31
  306.3 0.8 copy.29
  (10 shorter events, 0.1 us)
Async XLA Ops:
  7.2 108.9 %all-gather.2.cloned.1.call-start = ((), (), s32[]{:S(2)}) async-start(), calls=%async_computation.3 | async-start | bytes 8912896 | tf_op jit(solution)/shard_map/all_gather | solution.py:67
  7.9 242.6 %reduce-scatter.2.cloned.1.call-start = ((), (), s32[]{:S(2)}) async-start(), calls=%async_computation.4 | async-start | bytes 8912896 | tf_op jit(solution)/shard_map/reduce_scatter | solution.py:89
  10.0 1.6 copy-start
  10.0 106.1 %copy-start.2 = (bf16[128,512]{1,0:T(8,128)(2,1)S(1)}, bf16[128,512]{1,0:T(8,128)(2,1)}, u32[]{:S(2)}) copy-start(bf16[128,512]{1,0:T(8,128)(2,1)} %param.10) | copy-start | bytes 393220
  10.0 106.1 %copy-start.3 = (f32[8192]{0:T(1024)S(1)}, f32[8192]{0:T(1024)}, u32[]{:S(2)}) copy-start(f32[8192]{0:T(1024)} %param.9) | copy-start | bytes 98308
  116.1 6.5 %copy-start.1 = (bf16[128,8192]{1,0:T(8,128)(2,1)S(1)}, bf16[128,8192]{1,0:T(8,128)(2,1)}, u32[]{:S(2)}) copy-start(bf16[128,8192]{1,0:T(8,128)(2,1)} %param.8) | copy-start | bytes 6291460
  154.4 125.7 %copy-start.5 = (f32[16,1024]{1,0:T(8,128)S(1)}, f32[16,1024]{1,0:T(8,128)}, u32[]{:S(2)}) copy-start(f32[16,1024]{1,0:T(8,128)} %param.13) | copy-start | bytes 196612
  154.4 125.7 %copy-start.6 = (f32[16,1024]{1,0:T(8,128)S(1)}, f32[16,1024]{1,0:T(8,128)}, u32[]{:S(2)}) copy-start(f32[16,1024]{1,0:T(8,128)} %param.14) | copy-start | bytes 196612
  250.5 29.5 %all-to-all-start = ((bf16[16,16,1024]{2,1,0:T(8,128)(2,1)}), bf16[16,16,1024]{2,1,0:T(8,128)(2,1)S(1)}, u32[]{:S(2)}, u32[]{:S(2)}) async-start(bf16[16,16,1024]{2,1,0:T(8,128)(2,1)} %bitcast.31), calls=%async_computation.1 | async-start | bytes 1048576 | tf_op jit(solution)/shard_map/all_to_all | solution.py:25
  282.1 1.3 copy-start.4
  284.9 21.4 %all-to-all-start.1 = ((bf16[16,32,512]{2,1,0:T(8,128)(2,1)}), bf16[16,32,512]{2,1,0:T(8,128)(2,1)S(1)}, u32[]{:S(2)}, u32[]{:S(2)}) async-start(bf16[16,32,512]{2,1,0:T(8,128)(2,1)} %broadcast_in_dim.2), calls=%async_computation.2 | async-start | bytes 1048576 | tf_op jit(solution)/shard_map/all_to_all | solution.py:31
Sparse Core Ops, SparseCore 0:
  9.8 106.2 all-gather.1
  154.5 95.9 reduce-scatter.1
where the time goes:
time: 314 us
  waiting for transfers between devices  223 us (71%)
  starting transfers between devices  23.6 us (8%)
  matrix products  19.7 us (6%)
  other arithmetic  18.3 us (6%)
  local copies, waits for them, and re-layouts  15.2 us (5%)
  between operations  14.2 us (5%)
    all_gather x1, waiting for transfers between devices, shards(): gathered = lax.all_gather(secondary, 'node', axis=0, tiled=True)  104 us
    reduce_scatter x1, waiting for transfers between devices, shards(): lax.psum_scatter(joined.reshape(amount, 2 * key_width).astype(jnp.bfloat1...  96.1 us
    all_to_all x1, starting transfers between devices, sent_and_summed(): blocks = lax.all_to_all(split_up(value, dim, peers), axis, 0, 0, tiled=True)  15.8 us
    all_to_all x1, waiting for transfers between devices, sent_and_summed(): blocks = lax.all_to_all(split_up(value, dim, peers), axis, 0, 0, tiled=True)  13.7 us
    another operation x2, local copies, waits for them, and re-layouts  10.8 us
    all_to_all x1, waiting for transfers between devices, sent_to_all(): return lax.all_to_all(copies, axis, split_axis=0, concat_axis=0, tiled=True)  8.4 us
    concatenate x1, other arithmetic, shards(): jnp.concatenate([halves[0] + halves[1], halves[0] - halves[1]], axis=-1)  7.88 us
    all_to_all x1, starting transfers between devices, sent_to_all(): return lax.all_to_all(copies, axis, split_axis=0, concat_axis=0, tiled=True)  7.7 us
  transfers between devices with their start and end apart: 4, of which 4 were waited for; matrix products, arithmetic and copies ran while one was open for 3% of the time, Pallas kernels for 0%

commit v1 on v0

--- a/solution.py
+++ b/solution.py
@@ -64,7 +64,9 @@
     inverse = lax.rsqrt(jnp.mean(floats * floats, axis=-1, keepdims=True) + norm_eps)
     normed = floats * inverse
     hidden = (normed * norm_gain).astype(jnp.bfloat16)
-    gathered = lax.all_gather(secondary, "node", axis=0, tiled=True)
+    gathered = jnp.concatenate(
+        lax.all_to_all(jnp.stack([secondary] * lax.axis_size("node")), "node", 0, 0), axis=0
+    )
     keys = jnp.dot(hidden, gathered, preferred_element_type=jnp.float32).astype(jnp.bfloat16)
     hidden_grad = lax.dot_general(
         key_cotangent, gathered, (((1,), (1,)), ((), ())), preferred_element_type=jnp.float32

time: 314 us -> 407 us (1.30)
  waiting for transfers between devices: 223 us -> 303 us
  starting transfers between devices: 23.6 us -> 32.6 us
  local copies, waits for them, and re-layouts: 15.2 us -> 20.3 us
    all_to_all x0 -> x1, waiting for transfers between devices: none -> 149 us  [shards(): lax.all_to_all(jnp.stack([secondary] * lax.axis_size('node')), 'node', 0, 0)]
    all_gather x1 -> x0, waiting for transfers between devices: 104 us -> none  [shards(): gathered = lax.all_gather(secondary, 'node', axis=0, tiled=True)]
    reduce_scatter x1, waiting for transfers between devices: 96.1 us -> 132 us  [shards(): lax.psum_scatter(joined.reshape(amount, 2 * key_width).astype(jnp.bfloat1...]
    all_to_all x0 -> x1, starting transfers between devices: none -> 9.37 us  [shards(): lax.all_to_all(jnp.stack([secondary] * lax.axis_size('node')), 'node', 0, 0)]
    another operation x2 -> x3, local copies, waits for them, and re-layouts: 10.8 us -> 15.9 us
  transfers between devices with their start and end apart: 4 -> 4, of which waited for: 4 -> 4; matrix products, arithmetic and copies ran while one was open for 3% -> 2% of each run, Pallas kernels for 0% -> 0%
where the time goes in v1:
time: 407 us; the launch traced here: 406 us
  waiting for transfers between devices  303 us (74%)
  starting transfers between devices  32.6 us (8%)
  local copies, waits for them, and re-layouts  20.3 us (5%)
  matrix products  19.7 us (5%)
  other arithmetic  16.7 us (4%)
  between operations  14.2 us (3%)
    all_to_all x1, waiting for transfers between devices, shards(): lax.all_to_all(jnp.stack([secondary] * lax.axis_size('node')), 'node', 0, 0)  149 us
    reduce_scatter x1, waiting for transfers between devices, shards(): lax.psum_scatter(joined.reshape(amount, 2 * key_width).astype(jnp.bfloat1...  132 us
    all_to_all x1, starting transfers between devices, sent_and_summed(): blocks = lax.all_to_all(split_up(value, dim, peers), axis, 0, 0, tiled=True)  15.2 us
    all_to_all x1, waiting for transfers between devices, sent_and_summed(): blocks = lax.all_to_all(split_up(value, dim, peers), axis, 0, 0, tiled=True)  13.7 us
    another operation x2, local copies, waits for them, and re-layouts  10.8 us
    all_to_all x1, starting transfers between devices, shards(): lax.all_to_all(jnp.stack([secondary] * lax.axis_size('node')), 'node', 0, 0)  9.37 us
    all_to_all x1, waiting for transfers between devices, sent_to_all(): return lax.all_to_all(copies, axis, split_axis=0, concat_axis=0, tiled=True)  8.4 us
  transfers between devices with their start and end apart: 4, of which 4 were waited for; matrix products, arithmetic and copies ran while one was open for 2% of the time, Pallas kernels for 0%

profile of v1, /device:TPU:1, one launch (start us, length us, event | category | flops | bytes accessed | tf_op | source)
XLA Modules:
  0.0 406.1 jit_solution(3157900160021128071)
XLA Ops:
  7.2 5.1 %stack.8 = bf16[16,512,512]{2,1,0:T(8,128)(2,1)} broadcast(bf16[512,512]{1,0:T(8,128)(2,1)} %param.11), dimensions={1,2} | broadcast | bytes 8912896 | tf_op jit(solution)/shard_map/stack | solution.py:68
  12.3 0.0 copy-start.7
  12.3 0.0 copy-start.2
  12.3 9.4 %all-to-all-start = ((bf16[16,512,512]{2,1,0:T(8,128)(2,1)}), bf16[16,512,512]{2,1,0:T(8,128)(2,1)}, u32[]{:S(2)}, u32[]{:S(2)}) async-start(bf16[16,512,512]{2,1,0:T(8,128)(2,1)} %stack.8), calls=%async_computation | async-start | bytes 16777216 | tf_op jit(solution)/shard_map/all_to_all | solution.py:68
  21.6 0.0 reduce-scatter.2.cloned.1.call-start
  21.7 0.0 copy-done.7
  21.7 0.0 copy-done.2
  21.7 0.3 broadcast_multiply_fusion
  22.0 0.1 mul.382
  22.2 0.0 copy-start
  22.2 0.0 copy-start.3
  22.2 1.4 fusion.11
  23.6 0.1 reshape.203
  23.7 0.0 copy-done
  23.8 0.5 fusion.8
  24.3 148.6 %all-to-all-done = bf16[16,512,512]{2,1,0:T(8,128)(2,1)} async-done(((bf16[16,512,512]{2,1,0:T(8,128)(2,1)}), bf16[16,512,512]{2,1,0:T(8,128)(2,1)}, u32[]{:S(2)}, u32[]{:S(2)}) %all-to-all-start) | async-done | bytes 8388640 | tf_op jit(solution)/shard_map/all_to_all | solution.py:68
  172.9 0.0 copy-done.3
  172.9 0.0 copy-start.1
  172.9 6.5 %fusion.4 = (f32[128]{0:T(128)S(1)}, f32[128,8192]{1,0:T(8,128)S(1)}) fusion(bf16[128,8192]{1,0:T(8,128)(2,1)S(1)} %copy-done, f32[128]{0:T(128)S(1)} %add_rsqrt_fusion, f32[8192]{0:T(1024)S(1)} %copy-done.3, bf16[128,512]{1,0:T(8,128)(2,1)S(1)} %copy-done.2, bf16[8192,512]{1,0:T(8,128)(2,1)} %bitcast), kind=kOutput, calls=%fused_computation.10 | convolution fusion | flops 1078984576 | bytes 14844928 | tf_op jit(solution)/shard_map/dot_general | solution.py:71
  179.4 0.0 copy-done.1
  179.4 2.5 fusion.7
  181.9 2.5 copy.16
  184.4 3.9 fusion.9
  188.4 4.1 %add_convert_fusion = (bf16[1,256,16,512]{3,1,2,0:T(8,128)(2,1)}, bf16[1,256,16,512]{3,1,2,0:T(8,128)(2,1)S(1)}) fusion(f32[2,256,16,512]{3,1,2,0:T(8,128)S(1)} %fusion.9), kind=kLoop, calls=%fused_computation.3 | loop fusion | flops 8388608 | bytes 25165824 | tf_op jit(solution)/shard_map/convert.3
  192.5 6.5 %copy.19 = bf16[1,256,16,512]{3,2,1,0:T(8,128)(2,1)} copy(bf16[1,256,16,512]{3,1,2,0:T(8,128)(2,1)} %get-tuple-element.11) | data formatting | bytes 8388608 | tf_op jit(solution)/shard_map/convert.3
  199.0 4.3 %copy.20 = bf16[1,256,16,512]{3,2,1,0:T(8,128)(2,1)} copy(bf16[1,256,16,512]{3,1,2,0:T(8,128)(2,1)S(1)} %get-tuple-element.12) | data formatting | bytes 8388608 | tf_op jit(solution)/shard_map/convert.2
  203.3 7.9 %pad_maximum_fusion = bf16[4096,1024]{1,0:T(8,128)(2,1)} fusion(bf16[4096,512]{1,0:T(8,128)(2,1)} %bitcast.28, bf16[4096,512]{1,0:T(8,128)(2,1)} %bitcast.27), kind=kLoop, calls=%fused_computation.1 | loop fusion | flops 16777216 | bytes 16777216 | tf_op jit(solution)/shard_map/concatenate | solution.py:90
  211.2 0.0 copy-start.5
  211.2 0.0 copy-start.6
  211.2 0.0 reduce-scatter.2.cloned.1.call-update
  211.2 131.8 %reduce-scatter.2.cloned.1.call-done = bf16[256,1024]{1,0:T(8,128)(2,1)} async-done(((bf16[4096,1024]{1,0:T(8,128)(2,1)}), bf16[256,1024]{1,0:T(8,128)(2,1)}) %reduce-scatter.2.cloned.1.call-update) | async-done | bytes 524304 | tf_op jit(solution)/shard_map/reduce_scatter | solution.py:91
  343.0 15.2 %all-to-all-start.1 = ((bf16[16,16,1024]{2,1,0:T(8,128)(2,1)}), bf16[16,16,1024]{2,1,0:T(8,128)(2,1)S(1)}, u32[]{:S(2)}, u32[]{:S(2)}) async-start(bf16[16,16,1024]{2,1,0:T(8,128)(2,1)} %bitcast.32), calls=%async_computation.2 | async-start | bytes 1048576 | tf_op jit(solution)/shard_map/all_to_all | solution.py:25
  358.2 13.7 %all-to-all-done.1 = bf16[16,16,1024]{2,1,0:T(8,128)(2,1)S(1)} async-done(((bf16[16,16,1024]{2,1,0:T(8,128)(2,1)}), bf16[16,16,1024]{2,1,0:T(8,128)(2,1)S(1)}, u32[]{:S(2)}, u32[]{:S(2)}) %all-to-all-start.1) | async-done | bytes 524320 | tf_op jit(solution)/shard_map/all_to_all | solution.py:25
  371.9 0.1 convert_reduce_fusion
  372.0 0.0 copy-done.5
  372.0 0.0 copy-done.6
  372.0 0.7 add_divide_fusion
  372.7 1.3 fusion.13
  374.0 0.0 copy-start.4
  374.0 1.3 fusion.12
  375.3 0.0 copy-done.4
  375.3 0.6 fusion.42
  376.0 0.8 broadcast_in_dim.2
  376.8 7.9 %all-to-all-start.2 = ((bf16[16,32,512]{2,1,0:T(8,128)(2,1)}), bf16[16,32,512]{2,1,0:T(8,128)(2,1)S(1)}, u32[]{:S(2)}, u32[]{:S(2)}) async-start(bf16[16,32,512]{2,1,0:T(8,128)(2,1)} %broadcast_in_dim.2), calls=%async_computation.3 | async-start | bytes 1048576 | tf_op jit(solution)/shard_map/all_to_all | solution.py:31
  384.7 5.3 %convolution_convert_fusion = bf16[128,512]{1,0:T(8,128)(2,1)} fusion(bf16[128,8192]{1,0:T(8,128)(2,1)S(1)} %get-tuple-element.14, bf16[8192,512]{1,0:T(8,128)(2,1)} %bitcast), kind=kOutput, calls=%fused_computation.22 | convolution fusion | flops 1073807360 | bytes 10616832 | tf_op jit(solution)/shard_map/dot_general | solution.py:70
  390.0 8.4 %all-to-all-done.2 = bf16[16,32,512]{2,1,0:T(8,128)(2,1)S(1)} async-done(((bf16[16,32,512]{2,1,0:T(8,128)(2,1)}), bf16[16,32,512]{2,1,0:T(8,128)(2,1)S(1)}, u32[]{:S(2)}, u32[]{:S(2)}) %all-to-all-start.2) | async-done | bytes 524320 | tf_op jit(solution)/shard_map/all_to_all | solution.py:31
  398.4 0.8 copy.29
  (11 shorter events, 0.1 us)
Async XLA Ops:
  12.3 9.4 %copy-start.7 = (s32[1024]{0:T(1024)S(1)}, s32[1024]{0:T(1024)}, u32[]{:S(2)}) copy-start(s32[1024]{0:T(1024)} %param.15) | copy-start | bytes 12292
  12.3 9.5 %copy-start.2 = (bf16[128,512]{1,0:T(8,128)(2,1)S(1)}, bf16[128,512]{1,0:T(8,128)(2,1)}, u32[]{:S(2)}) copy-start(bf16[128,512]{1,0:T(8,128)(2,1)} %param.10) | copy-start | bytes 393220
  12.3 160.6 %all-to-all-start = ((bf16[16,512,512]{2,1,0:T(8,128)(2,1)}), bf16[16,512,512]{2,1,0:T(8,128)(2,1)}, u32[]{:S(2)}, u32[]{:S(2)}) async-start(bf16[16,512,512]{2,1,0:T(8,128)(2,1)} %stack.8), calls=%async_computation | async-start | bytes 16777216 | tf_op jit(solution)/shard_map/all_to_all | solution.py:68
  21.6 321.3 %reduce-scatter.2.cloned.1.call-start = ((), (), s32[]{:S(2)}) async-start(), calls=%async_computation.4 | async-start | bytes 8912896 | tf_op jit(solution)/shard_map/reduce_scatter | solution.py:91
  22.2 1.6 copy-start
  22.2 150.7 %copy-start.3 = (f32[8192]{0:T(1024)S(1)}, f32[8192]{0:T(1024)}, u32[]{:S(2)}) copy-start(f32[8192]{0:T(1024)} %param.9) | copy-start | bytes 98308
  172.9 6.5 %copy-start.1 = (bf16[128,8192]{1,0:T(8,128)(2,1)S(1)}, bf16[128,8192]{1,0:T(8,128)(2,1)}, u32[]{:S(2)}) copy-start(bf16[128,8192]{1,0:T(8,128)(2,1)} %param.8) | copy-start | bytes 6291460
  211.2 160.8 %copy-start.5 = (f32[16,1024]{1,0:T(8,128)S(1)}, f32[16,1024]{1,0:T(8,128)}, u32[]{:S(2)}) copy-start(f32[16,1024]{1,0:T(8,128)} %param.13) | copy-start | bytes 196612
  211.2 160.8 %copy-start.6 = (f32[16,1024]{1,0:T(8,128)S(1)}, f32[16,1024]{1,0:T(8,128)}, u32[]{:S(2)}) copy-start(f32[16,1024]{1,0:T(8,128)} %param.14) | copy-start | bytes 196612
  343.0 28.9 %all-to-all-start.1 = ((bf16[16,16,1024]{2,1,0:T(8,128)(2,1)}), bf16[16,16,1024]{2,1,0:T(8,128)(2,1)S(1)}, u32[]{:S(2)}, u32[]{:S(2)}) async-start(bf16[16,16,1024]{2,1,0:T(8,128)(2,1)} %bitcast.32), calls=%async_computation.2 | async-start | bytes 1048576 | tf_op jit(solution)/shard_map/all_to_all | solution.py:25
  374.0 1.3 copy-start.4
  376.8 21.6 %all-to-all-start.2 = ((bf16[16,32,512]{2,1,0:T(8,128)(2,1)}), bf16[16,32,512]{2,1,0:T(8,128)(2,1)S(1)}, u32[]{:S(2)}, u32[]{:S(2)}) async-start(bf16[16,32,512]{2,1,0:T(8,128)(2,1)} %broadcast_in_dim.2), calls=%async_computation.3 | async-start | bytes 1048576 | tf_op jit(solution)/shard_map/all_to_all | solution.py:31
Sparse Core Ops, SparseCore 0:
  211.3 131.6 reduce-scatter.1
